TPU v7x, 32 devices: a whole 2x2x4 slice. The times are simulated.
32 devices in a mesh: row: 4 (over y, x), col: 8 (over z, core).
Axes of the slice: x: 2, y: 2, z: 4, core: 2. Of those that a mesh axis runs over, the one named last changes fastest.
Arguments:
- stiffness: float32 [12, 4, 128, 6144], P(None, 'row', None, 'col'), may hold values from -8 to 8
- lower_first: float32 [1024, 10, 4, 128], P('col', None, 'row'), may hold values from -0.1875 to 0.1875
- lower_second: float32 [1024, 8, 4, 128], P('col', None, 'row'), may hold values from -0.1875 to 0.1875
- diag_inv: float32 [2, 1024, 2, 4, 128], P(None, 'col', None, 'row'), as said below
Outputs:
- reduced: float32 [12, 4, 128, 6144], P(None, 'row', None, 'col')
Inputs may be any that keep to these rules, and one draw needn't show every extreme that they name: Each block of diag_inv, read as a 1024 x 1024 matrix, is zero above its diagonal and has a positive diagonal.
All inputs are finite; a program needn't handle non-finite values.
Results may differ from a plain program's by a relative error of at most 0.000086.
Values sent between devices are 32-bit elements; how exact they have to be, the bound alone decides.
A program may use at most 128 MiB of HBM per device.

v0:
```python
import jax
import jax.numpy as jnp
from jax import lax
from jax.sharding import PartitionSpec as P


def product(left, right):
    return jnp.dot(left, right, precision=lax.Precision.HIGH, preferred_element_type=jnp.float32)


def apply_cols(columns, factor):
    return lax.dot_general(
        columns,
        factor,
        (((0,), (0,)), ((), ())),
        precision=lax.Precision.HIGH,
        preferred_element_type=jnp.float32,
    )


def shards(stiffness, lower_first, lower_second, diag_inv):
    cycles = stiffness.shape[0]
    rblk = stiffness.shape[2]
    cdev = stiffness.shape[3]
    pcount = diag_inv.shape[2]
    nrow = lax.axis_size("row")
    nb = diag_inv.shape[1] * lax.axis_size("col")
    height = pcount * rblk
    matrix_rows = stiffness.reshape(cycles * rblk, cdev)
    inv_cols = lax.all_gather(diag_inv, "col", axis=1, tiled=True)
    inverse = inv_cols.reshape(2, nb, height)

    def own_rows(solved):
        grouped = solved.reshape(pcount, nrow, rblk, cdev)
        mine = lax.dynamic_slice_in_dim(grouped, lax.axis_index("row"), 1, 1)
        return mine.reshape(height, cdev)

    w_first = lax.psum(product(inverse[0], matrix_rows[:height]), "row")
    coupling = lax.all_gather(lower_first[:, :pcount], "col", axis=0, tiled=True).reshape(
        nb, height
    )
    w_second = lax.psum(
        product(inverse[1], matrix_rows[height : 2 * height] - apply_cols(coupling, w_first)), "row"
    )
    pieces = (
        lax.all_gather(lower_first[:, pcount:], "col", axis=0, tiled=True),
        lax.all_gather(lower_second, "col", axis=0, tiled=True),
    )
    count = pieces[0].shape[0]
    first_piece = pieces[0].reshape(count, -1)
    second_piece = pieces[1].reshape(count, -1)
    remain = (
        matrix_rows[2 * height :]
        - apply_cols(first_piece, w_first)
        - apply_cols(second_piece, w_second)
    )
    stacked = jnp.concatenate([own_rows(w_first), own_rows(w_second), remain], axis=0)
    return stacked.reshape(cycles, 1, rblk, cdev)


def solution(mesh):
    placed = (
        P(None, "row", None, "col"),
        P("col", None, "row", None),
        P("col", None, "row", None),
        P(None, "col", None, "row", None),
    )
    return jax.shard_map(
        shards, mesh=mesh, in_specs=placed, out_specs=P(None, "row", None, "col"), check_vma=False
    )
```

profile of v0, /device:TPU:0, one launch (start us, length us, event | category | flops | bytes accessed | tf_op | source)
XLA Modules:
  0.0 369.2 jit_solution(9611690720741950493)
XLA Ops:
  6.5 0.0 all-gather.5.cloned.1.call-start
  6.5 0.7 all-gather.5.cloned.1.call-update
  7.3 0.0 all-gather.7.cloned.1.call-start
  7.3 1.6 slice.37
  8.9 0.0 all-gather.7.cloned.1.call-update
  8.9 0.0 all-reduce.3.cloned.1.call-start
  8.9 1.5 fusion.16
  10.4 30.4 %all-gather.5.cloned.1.call-done = f32[2,1024,2,1,128]{4,3,2,1,0:T(1,128)} async-done(((f32[2,128,2,1,128]{4,3,2,1,0:T(1,128)}), f32[2,1024,2,1,128]{4,3,2,1,0:T(1,128)}) %all-gather.5.cloned.1.call-update) | async-done | bytes 2097168 | tf_op jit(solution)/shard_map/all_gather | solution.py:30
  40.8 7.8 %slice_reduce_fusion = (f32[1024,2,128]{2,1,0:T(2,128)S(1)}, f32[1024,2,128]{2,1,0:T(2,128)S(1)}) fusion(f32[2,1024,2,1,128]{4,3,2,1,0:T(1,128)} %all-gather.5.cloned.1.call-done), kind=kLoop, calls=%fused_computation.19 | loop fusion | bytes 4194304 | tf_op jit(solution)/shard_map/slice | solution.py:43
  48.7 3.1 fusion.13
  51.8 0.0 all-reduce.3.cloned.1.call-update
  51.8 0.0 all-reduce.5.cloned.1.call-start
  51.9 0.3 copy.21
  52.2 12.0 %all-gather.7.cloned.1.call-done = f32[1024,2,1,128]{3,1,2,0:T(2,128)} async-done(((f32[128,2,1,128]{3,1,2,0:T(2,128)}), f32[1024,2,1,128]{3,1,2,0:T(2,128)}) %all-gather.7.cloned.1.call-update) | async-done | bytes 1048592 | tf_op jit(solution)/shard_map/all_gather | solution.py:39
  64.1 89.7 %all-reduce.3.cloned.1.call-done = f32[1024,768]{1,0:T(8,128)} async-done(((f32[1024,768]{1,0:T(8,128)}), f32[1024,768]{1,0:T(8,128)}) %all-reduce.3.cloned.1.call-update) | async-done | bytes 3145744 | tf_op jit(solution)/shard_map/psum | solution.py:38
  153.8 4.8 %fusion.8 = f32[256,768]{0,1:T(8,128)S(1)} fusion(f32[256,768]{0,1:T(8,128)S(1)} %copy.21, f32[1024,768]{1,0:T(8,128)} %all-reduce.3.cloned.1.call-done, f32[128,8,2,128]{3,2,1,0:T(2,128)} %bitcast.76), kind=kOutput, calls=%fused_computation.11 | convolution fusion | flops 1208156160 | bytes 5767168 | tf_op jit(solution)/shard_map/dot_general | solution.py:12
  158.6 0.0 copy-start.3
  158.6 3.1 convolution_bitcast_fusion
  161.7 0.0 all-reduce.5.cloned.1.call-update
  161.7 0.0 all-gather.11.cloned.1.call-start
  161.8 0.5 all-gather.11.cloned.1.call-update
  162.3 0.2 all-gather.9.cloned.1.call-start
  162.5 0.0 copy-done.3
  162.6 0.8 slice.41
  163.4 0.0 all-gather.9.cloned.1.call-update
  163.4 3.8 %slice.39 = f32[8,1,128,768]{3,2,1,0:T(8,128)} slice(f32[12,1,128,768]{3,2,1,0:T(8,128)} %param.4), slice={[4:12], [0:1], [0:128], [0:768]} | slice | bytes 6291456 | tf_op jit(solution)/shard_map/slice | solution.py:53
  167.2 0.0 copy-start
  167.2 4.1 %copy.22 = f32[1024,768]{0,1:T(8,128)} copy(f32[1024,768]{1,0:T(8,128)} %bitcast.65) | data formatting | bytes 6291456 | tf_op jit(solution)/shard_map/slice | solution.py:53
  171.3 0.0 copy-done
  171.3 0.9 constant_dynamic-slice_fusion
  172.3 2.3 copy.20
  174.6 74.3 %all-reduce.5.cloned.1.call-done = f32[1024,768]{0,1:T(8,128)} async-done(((f32[1024,768]{0,1:T(8,128)}), f32[1024,768]{0,1:T(8,128)}) %all-reduce.5.cloned.1.call-update) | async-done | bytes 3145744 | tf_op jit(solution)/shard_map/psum | solution.py:42
  248.8 5.1 %reshape.36 = f32[2,4,128,768]{2,1,0,3:T(4,128)} reshape(f32[1024,768]{0,1:T(8,128)} %all-reduce.5.cloned.1.call-done) | data formatting | bytes 6291456 | tf_op jit(solution)/shard_map/reshape | solution.py:34
  254.0 4.6 %dynamic-slice_reduce_fusion = f32[2,128,768]{1,0,2:T(2,128)S(1)} fusion(f32[2,4,128,768]{2,1,0,3:T(4,128)} %reshape.36, s32[]{:T(128)S(6)} %select_n.4), kind=kLoop, calls=%fused_computation.22 | loop fusion | bytes 1572868 | tf_op jit(solution)/shard_map/dynamic_slice | solution.py:35
  258.5 0.9 copy.54
  259.5 37.7 %all-gather.11.cloned.1.call-done = f32[1024,8,1,128]{3,1,2,0:T(8,128)} async-done(((f32[128,8,1,128]{3,1,2,0:T(8,128)}), f32[1024,8,1,128]{3,1,2,0:T(8,128)}) %all-gather.11.cloned.1.call-update) | async-done | bytes 4194320 | tf_op jit(solution)/shard_map/all_gather | solution.py:47
  297.2 9.6 %fusion = f32[768,1024]{1,0:T(8,128)} fusion(f32[1024,768]{0,1:T(8,128)} %all-reduce.5.cloned.1.call-done, f32[128,8,8,128]{3,2,1,0:T(8,128)} %bitcast.66), kind=kOutput, calls=%fused_computation.1 | convolution fusion | flops 4831838208 | bytes 10485760 | tf_op jit(solution)/shard_map/dot_general | solution.py:12
  306.8 37.6 %all-gather.9.cloned.1.call-done = f32[1024,8,1,128]{3,1,2,0:T(8,128)} async-done(((f32[128,8,1,128]{3,1,2,0:T(8,128)}), f32[1024,8,1,128]{3,1,2,0:T(8,128)}) %all-gather.9.cloned.1.call-update) | async-done | bytes 4194320 | tf_op jit(solution)/shard_map/all_gather | solution.py:46
  344.3 0.0 copy-start.1
  344.3 0.0 copy-start.2
  344.3 9.4 %bitcast_subtract_fusion = f32[1024,768]{0,1:T(8,128)S(1)} fusion(f32[768,1024]{1,0:T(8,128)} %fusion, f32[1024,768]{0,1:T(8,128)} %copy.22, f32[1024,768]{1,0:T(8,128)S(1)} %copy-done, f32[128,8,8,128]{3,2,1,0:T(8,128)} %bitcast.69), kind=kOutput, calls=%fused_computation.7 | convolution fusion | flops 4833411072 | bytes 16777216 | tf_op jit(solution)/shard_map/dot_general | solution.py:12
  353.7 0.0 copy-done.1
  353.8 0.0 copy-done.2
  353.8 2.6 pad_maximum_fusion
  356.4 6.0 %copy.18 = f32[1536,768]{1,0:T(8,128)} copy(f32[1536,768]{0,1:T(8,128)} %pad_maximum_fusion) | data formatting | bytes 9437184 | tf_op jit(solution)/shard_map/concatenate | solution.py:57
Async XLA Ops:
  6.5 34.3 %all-gather.5.cloned.1.call-start = ((), (), s32[]{:S(2)}) async-start(), calls=%async_computation | async-start | bytes 2359296 | tf_op jit(solution)/shard_map/all_gather | solution.py:30
  7.3 56.9 %all-gather.7.cloned.1.call-start = ((), (), s32[]{:S(2)}) async-start(), calls=%async_computation.2 | async-start | bytes 1179648 | tf_op jit(solution)/shard_map/all_gather | solution.py:39
  8.9 144.9 %all-reduce.3.cloned.1.call-start = ((), (), s32[]{:S(2)}) async-start(), calls=%async_computation.1 | async-start | bytes 6291456 | tf_op jit(solution)/shard_map/psum | solution.py:38
  51.8 197.0 %all-reduce.5.cloned.1.call-start = ((), (), s32[]{:S(2)}) async-start(), calls=%async_computation.3 | async-start | bytes 6291456 | tf_op jit(solution)/shard_map/psum | solution.py:42
  158.6 4.0 %copy-start.3 = (f32[128,10,1,128]{3,2,1,0:T(1,128)S(1)}, f32[128,10,1,128]{3,2,1,0:T(1,128)}, u32[]{:S(2)}) copy-start(f32[128,10,1,128]{3,2,1,0:T(1,128)} %param.5) | copy-start | bytes 1966084
  161.7 135.4 %all-gather.11.cloned.1.call-start = ((), (), s32[]{:S(2)}) async-start(), calls=%async_computation.5 | async-start | bytes 4718592 | tf_op jit(solution)/shard_map/all_gather | solution.py:47
  162.3 182.0 %all-gather.9.cloned.1.call-start = ((), (), s32[]{:S(2)}) async-start(), calls=%async_computation.4 | async-start | bytes 4718592 | tf_op jit(solution)/shard_map/all_gather | solution.py:46
  167.2 4.1 %copy-start = (f32[1024,768]{1,0:T(8,128)S(1)}, f32[1024,768]{1,0:T(8,128)}, u32[]{:S(2)}) copy-start(f32[1024,768]{1,0:T(8,128)} %all-reduce.3.cloned.1.call-done) | copy-start | bytes 9437188
  344.3 9.4 %copy-start.1 = (f32[256,768]{0,1:T(8,128)S(1)}, f32[256,768]{0,1:T(8,128)}, u32[]{:S(2)}) copy-start(f32[256,768]{0,1:T(8,128)} %copy.20) | copy-start | bytes 2359300
  344.3 9.4 %copy-start.2 = (f32[96,8,2,128]{3,1,2,0:T(8,128)S(1)}, f32[96,8,2,128]{3,1,2,0:T(8,128)}, u32[]{:S(2)}) copy-start(f32[96,8,2,128]{3,1,2,0:T(8,128)} %copy.54) | copy-start | bytes 2359300
Sparse Core Ops, SparseCore 0:
  8.9 31.8 all-gather.4
  42.4 21.6 all-gather.6
  67.2 86.5 all-reduce.2
  161.9 86.9 all-reduce.4
  250.3 46.8 all-gather.10
  298.6 45.6 all-gather.8
where the time goes:
time: 370 us; the launch traced here: 369 us
  waiting for transfers between devices  283 us (76%)
  local copies, waits for them, and re-layouts  39.8 us (11%)
  matrix products  30 us (8%)
  between operations  13.6 us (4%)
    psum x1, waiting for transfers between devices, shards(): w_first = lax.psum(product(inverse[0], matrix_rows[:height]), 'row')  89.7 us
    psum x1, waiting for transfers between devices, shards(): lax.psum(product(inverse[1], matrix_rows[height:2 * height] - apply_cols(...  74.3 us
    all_gather x1, waiting for transfers between devices, shards(): lax.all_gather(lower_second, 'col', axis=0, tiled=True)  37.7 us
    all_gather x1, waiting for transfers between devices, shards(): lax.all_gather(lower_first[:, pcount:], 'col', axis=0, tiled=True)  37.6 us
    all_gather x1, waiting for transfers between devices, shards(): inv_cols = lax.all_gather(diag_inv, 'col', axis=1, tiled=True)  30.4 us
    dot_general x3, matrix products, apply_cols(): lax.dot_general(columns, factor, (((0,), (0,)), ((), ())), precision=lax....  23.8 us
    all_gather x1, waiting for transfers between devices, shards(): lax.all_gather(lower_first[:, :pcount], 'col', axis=0, tiled=True)  12 us
    slice x2, local copies, waits for them, and re-layouts, shards(): matrix_rows[2 * height:] - apply_cols(first_piece, w_first)  7.89 us
  transfers between devices with their start and end apart: 6, of which 6 were waited for; matrix products, arithmetic and copies ran while one was open for 13% of the time, Pallas kernels for 0%

commit v1 on v0

--- a/solution.py
+++ b/solution.py
@@ -27,7 +27,9 @@
     nb = diag_inv.shape[1] * lax.axis_size("col")
     height = pcount * rblk
     matrix_rows = stiffness.reshape(cycles * rblk, cdev)
-    inv_cols = lax.all_gather(diag_inv, "col", axis=1, tiled=True)
+    inv_cols = jnp.concatenate(
+        lax.all_to_all(jnp.stack([diag_inv] * lax.axis_size("col")), "col", 0, 0), axis=1
+    )
     inverse = inv_cols.reshape(2, nb, height)
 
     def own_rows(solved):

time: 370 us -> 311 us (0.84)
  waiting for transfers between devices: 283 us -> 213 us
  starting transfers between devices: 0.39 us -> 6.74 us
  local copies, waits for them, and re-layouts: 39.8 us -> 43.8 us
    all_to_all x0 -> x1, waiting for transfers between devices: none -> 53 us  [shards(): lax.all_to_all(jnp.stack([diag_inv] * lax.axis_size('col')), 'col', 0, 0)]
    all_gather x1, waiting for transfers between devices: 37.7 us -> 0.01 us  [shards(): lax.all_gather(lower_second, 'col', axis=0, tiled=True)]
    all_gather x1, waiting for transfers between devices: 37.6 us -> 0.01 us  [shards(): lax.all_gather(lower_first[:, pcount:], 'col', axis=0, tiled=True)]
    all_gather x1 -> x0, waiting for transfers between devices: 30.4 us -> none  [shards(): inv_cols = lax.all_gather(diag_inv, 'col', axis=1, tiled=True)]
    all_gather x1, waiting for transfers between devices: 12 us -> 0.02 us  [shards(): lax.all_gather(lower_first[:, :pcount], 'col', axis=0, tiled=True)]
    all_to_all x0 -> x1, starting transfers between devices: none -> 6.35 us  [shards(): lax.all_to_all(jnp.stack([diag_inv] * lax.axis_size('col')), 'col', 0, 0)]
    psum x1, waiting for transfers between devices: 89.7 us -> 85.3 us  [shards(): w_first = lax.psum(product(inverse[0], matrix_rows[:height]), 'row')]
    another operation x0 -> x1, local copies, waits for them, and re-layouts: none -> 3.88 us  [shards(): jnp.stack([diag_inv] * lax.axis_size('col'))]
  transfers between devices with their start and end apart: 6 -> 6, of which waited for: 6 -> 3; matrix products, arithmetic and copies ran while one was open for 13% -> 15% of each run, Pallas kernels for 0% -> 0%
where the time goes in v1:
time: 311 us
  waiting for transfers between devices  213 us (68%)
  local copies, waits for them, and re-layouts  43.8 us (14%)
  matrix products  30 us (10%)
  between operations  14.7 us (5%)
  starting transfers between devices  6.74 us (2%)
    psum x1, waiting for transfers between devices, shards(): w_first = lax.psum(product(inverse[0], matrix_rows[:height]), 'row')  85.3 us
    psum x1, waiting for transfers between devices, shards(): lax.psum(product(inverse[1], matrix_rows[height:2 * height] - apply_cols(...  73.7 us
    all_to_all x1, waiting for transfers between devices, shards(): lax.all_to_all(jnp.stack([diag_inv] * lax.axis_size('col')), 'col', 0, 0)  53 us
    dot_general x3, matrix products, apply_cols(): lax.dot_general(columns, factor, (((0,), (0,)), ((), ())), precision=lax....  23.8 us
    slice x2, local copies, waits for them, and re-layouts, shards(): matrix_rows[2 * height:] - apply_cols(first_piece, w_first)  7.83 us
    slice x1, local copies, waits for them, and re-layouts, shards(): inverse[1]  6.6 us
    all_to_all x1, starting transfers between devices, shards(): lax.all_to_all(jnp.stack([diag_inv] * lax.axis_size('col')), 'col', 0, 0)  6.35 us
  transfers between devices with their start and end apart: 6, of which 3 were waited for; matrix products, arithmetic and copies ran while one was open for 15% of the time, Pallas kernels for 0%

profile of v1, /device:TPU:0, one launch (start us, length us, event | category | flops | bytes accessed | tf_op | source)
XLA Modules:
  0.0 310.8 jit_solution(15696055227488575447)
XLA Ops:
  7.4 3.9 %stack.2 = f32[8,2,128,2,1,128]{5,4,3,2,1,0:T(1,128)} broadcast(f32[2,128,2,128]{3,2,1,0:T(2,128)} %bitcast.84), dimensions={1,2,3,5} | broadcast | bytes 2359296 | tf_op jit(solution)/shard_map/stack | solution.py:31
  11.3 6.4 %all-to-all-start = ((f32[8,2,128,2,1,128]{5,4,3,2,1,0:T(1,128)}), f32[8,2,128,2,1,128]{5,4,3,2,1,0:T(1,128)S(1)}, u32[]{:S(2)}, u32[]{:S(2)}) async-start(f32[8,2,128,2,1,128]{5,4,3,2,1,0:T(1,128)} %stack.2), calls=%async_computation | async-start | bytes 4194304 | tf_op jit(solution)/shard_map/all_to_all | solution.py:31
  17.6 0.0 all-gather.4.cloned.1.call-start
  17.7 1.6 slice.37
  19.2 0.0 all-gather.4.cloned.1.call-update
  19.2 0.0 all-reduce.3.cloned.1.call-start
  19.3 2.7 fusion.16
  22.0 53.0 %all-to-all-done = f32[8,2,128,2,1,128]{5,4,3,2,1,0:T(1,128)S(1)} async-done(((f32[8,2,128,2,1,128]{5,4,3,2,1,0:T(1,128)}), f32[8,2,128,2,1,128]{5,4,3,2,1,0:T(1,128)S(1)}, u32[]{:S(2)}, u32[]{:S(2)}) %all-to-all-start) | async-done | bytes 2097184 | tf_op jit(solution)/shard_map/all_to_all | solution.py:31
  75.1 0.0 copy-start.3
  75.1 6.6 %slice_reduce_fusion = (f32[8,128,2,128]{3,2,1,0:T(2,128)S(1)}, f32[8,128,2,128]{3,2,1,0:T(2,128)S(1)}) fusion(f32[2,8,128,2,1,128]{5,4,3,2,0,1:T(1,128)S(1)} %bitcast.70), kind=kLoop, calls=%fused_computation.19 | loop fusion | bytes 4194304 | tf_op jit(solution)/shard_map/slice | solution.py:45
  81.7 0.0 copy-done.3
  81.7 0.0 copy-start.4
  81.7 3.1 %fusion.13 = f32[1024,768]{1,0:T(8,128)} fusion(f32[256,768]{1,0:T(8,128)S(1)} %bitcast.76, f32[128,8,2,128]{3,2,1,0:T(2,128)S(1)} %bitcast.73), kind=kOutput, calls=%fused_computation.16 | convolution fusion | flops 1207959552 | bytes 4980736 | tf_op jit(solution)/shard_map/dot_general | solution.py:8
  84.8 0.0 all-reduce.3.cloned.1.call-update
  84.8 0.0 all-reduce.5.cloned.1.call-start
  84.9 0.0 copy-done.4
  84.9 0.3 copy.21
  85.2 0.0 all-gather.4.cloned.1.call-done
  85.2 85.3 %all-reduce.3.cloned.1.call-done = f32[1024,768]{1,0:T(8,128)} async-done(((f32[1024,768]{1,0:T(8,128)}), f32[1024,768]{1,0:T(8,128)}) %all-reduce.3.cloned.1.call-update) | async-done | bytes 3145744 | tf_op jit(solution)/shard_map/psum | solution.py:40
  170.5 4.8 %fusion.8 = f32[256,768]{0,1:T(8,128)S(1)} fusion(f32[256,768]{0,1:T(8,128)S(1)} %copy.21, f32[1024,768]{1,0:T(8,128)} %all-reduce.3.cloned.1.call-done, f32[128,8,2,128]{3,2,1,0:T(2,128)} %bitcast.81), kind=kOutput, calls=%fused_computation.11 | convolution fusion | flops 1208156160 | bytes 5767168 | tf_op jit(solution)/shard_map/dot_general | solution.py:12
  175.3 0.0 copy-start.5
  175.4 3.1 %convolution_bitcast_fusion = f32[1024,768]{0,1:T(8,128)} fusion(f32[256,768]{0,1:T(8,128)S(1)} %fusion.8, f32[128,8,2,128]{3,2,1,0:T(2,128)S(1)} %bitcast.72), kind=kOutput, calls=%fused_computation.9 | convolution fusion | flops 1207959552 | bytes 4980736 | tf_op jit(solution)/shard_map/dot_general | solution.py:8
  178.5 0.0 all-reduce.5.cloned.1.call-update
  178.5 0.0 all-gather.8.cloned.1.call-start
  178.5 0.7 all-gather.8.cloned.1.call-update
  179.2 0.2 all-gather.6.cloned.1.call-start
  179.5 0.0 copy-done.5
  179.5 0.8 slice.41
  180.3 0.0 all-gather.6.cloned.1.call-update
  180.3 3.8 %slice.39 = f32[8,1,128,768]{3,2,1,0:T(8,128)} slice(f32[12,1,128,768]{3,2,1,0:T(8,128)} %param.4), slice={[4:12], [0:1], [0:128], [0:768]} | slice | bytes 6291456 | tf_op jit(solution)/shard_map/slice | solution.py:55
  184.1 0.0 copy-start
  184.1 4.1 %copy.22 = f32[1024,768]{0,1:T(8,128)} copy(f32[1024,768]{1,0:T(8,128)} %bitcast.69) | data formatting | bytes 6291456 | tf_op jit(solution)/shard_map/slice | solution.py:55
  188.2 0.0 copy-done
  188.2 1.0 constant_dynamic-slice_fusion
  189.2 2.3 copy.20
  191.5 73.7 %all-reduce.5.cloned.1.call-done = f32[1024,768]{0,1:T(8,128)} async-done(((f32[1024,768]{0,1:T(8,128)}), f32[1024,768]{0,1:T(8,128)}) %all-reduce.5.cloned.1.call-update) | async-done | bytes 3145744 | tf_op jit(solution)/shard_map/psum | solution.py:44
  265.3 5.1 %reshape.42 = f32[2,4,128,768]{2,1,0,3:T(4,128)} reshape(f32[1024,768]{0,1:T(8,128)} %all-reduce.5.cloned.1.call-done) | data formatting | bytes 6291456 | tf_op jit(solution)/shard_map/reshape | solution.py:36
  270.4 4.6 %dynamic-slice_reduce_fusion = f32[2,128,768]{1,0,2:T(2,128)S(1)} fusion(f32[2,4,128,768]{2,1,0,3:T(4,128)} %reshape.42, s32[]{:T(128)S(6)} %select_n.4), kind=kLoop, calls=%fused_computation.22 | loop fusion | bytes 1572868 | tf_op jit(solution)/shard_map/dynamic_slice | solution.py:37
  275.0 1.0 copy.54
  275.9 0.0 all-gather.8.cloned.1.call-done
  275.9 9.6 %fusion = f32[768,1024]{1,0:T(8,128)} fusion(f32[1024,768]{0,1:T(8,128)} %all-reduce.5.cloned.1.call-done, f32[128,8,8,128]{3,2,1,0:T(8,128)} %bitcast.71), kind=kOutput, calls=%fused_computation.1 | convolution fusion | flops 4831838208 | bytes 10485760 | tf_op jit(solution)/shard_map/dot_general | solution.py:12
  285.5 0.0 all-gather.6.cloned.1.call-done
  285.6 0.0 copy-start.1
  285.6 9.4 %bitcast_subtract_fusion = f32[1024,768]{0,1:T(8,128)S(1)} fusion(f32[768,1024]{1,0:T(8,128)} %fusion, f32[1024,768]{0,1:T(8,128)} %copy.22, f32[1024,768]{1,0:T(8,128)S(1)} %copy-done, f32[128,8,8,128]{3,2,1,0:T(8,128)} %bitcast.74), kind=kOutput, calls=%fused_computation.7 | convolution fusion | flops 4833411072 | bytes 16777216 | tf_op jit(solution)/shard_map/dot_general | solution.py:12
  295.0 0.0 copy-done.1
  295.0 0.0 copy-done.2
  295.0 2.6 pad_maximum_fusion
  297.6 6.0 %copy.18 = f32[1536,768]{1,0:T(8,128)} copy(f32[1536,768]{0,1:T(8,128)} %pad_maximum_fusion) | data formatting | bytes 9437184 | tf_op jit(solution)/shard_map/concatenate | solution.py:59
  (1 shorter events, 0.0 us)
Async XLA Ops:
  11.3 63.8 %all-to-all-start = ((f32[8,2,128,2,1,128]{5,4,3,2,1,0:T(1,128)}), f32[8,2,128,2,1,128]{5,4,3,2,1,0:T(1,128)S(1)}, u32[]{:S(2)}, u32[]{:S(2)}) async-start(f32[8,2,128,2,1,128]{5,4,3,2,1,0:T(1,128)} %stack.2), calls=%async_computation | async-start | bytes 4194304 | tf_op jit(solution)/shard_map/all_to_all | solution.py:31
  17.6 67.6 %all-gather.4.cloned.1.call-start = ((), (), s32[]{:S(2)}) async-start(), calls=%async_computation.2 | async-start | bytes 1179648 | tf_op jit(solution)/shard_map/all_gather | solution.py:41
  19.2 151.3 %all-reduce.3.cloned.1.call-start = ((), (), s32[]{:S(2)}) async-start(), calls=%async_computation.1 | async-start | bytes 6291456 | tf_op jit(solution)/shard_map/psum | solution.py:40
  75.1 6.6 %copy-start.3 = (f32[2,1,128,768]{3,2,1,0:T(8,128)S(1)}, f32[2,1,128,768]{3,2,1,0:T(8,128)}, u32[]{:S(2)}) copy-start(f32[2,1,128,768]{3,2,1,0:T(8,128)} %get-tuple-element.7) | copy-start | bytes 2359300
  81.7 3.2 %copy-start.4 = (f32[2,1,128,768]{3,2,1,0:T(8,128)S(1)}, f32[2,1,128,768]{3,2,1,0:T(8,128)}, u32[]{:S(2)}) copy-start(f32[2,1,128,768]{3,2,1,0:T(8,128)} %get-tuple-element.8) | copy-start | bytes 2359300
  84.8 180.4 %all-reduce.5.cloned.1.call-start = ((), (), s32[]{:S(2)}) async-start(), calls=%async_computation.3 | async-start | bytes 6291456 | tf_op jit(solution)/shard_map/psum | solution.py:44
  175.3 4.1 %copy-start.5 = (f32[128,10,1,128]{3,2,1,0:T(1,128)S(1)}, f32[128,10,1,128]{3,2,1,0:T(1,128)}, u32[]{:S(2)}) copy-start(f32[128,10,1,128]{3,2,1,0:T(1,128)} %param.5) | copy-start | bytes 1966084
  178.5 97.5 %all-gather.8.cloned.1.call-start = ((), (), s32[]{:S(2)}) async-start(), calls=%async_computation.5 | async-start | bytes 4718592 | tf_op jit(solution)/shard_map/all_gather | solution.py:49
  179.2 106.3 %all-gather.6.cloned.1.call-start = ((), (), s32[]{:S(2)}) async-start(), calls=%async_computation.4 | async-start | bytes 4718592 | tf_op jit(solution)/shard_map/all_gather | solution.py:48
  184.1 4.1 %copy-start = (f32[1024,768]{1,0:T(8,128)S(1)}, f32[1024,768]{1,0:T(8,128)}, u32[]{:S(2)}) copy-start(f32[1024,768]{1,0:T(8,128)} %all-reduce.3.cloned.1.call-done) | copy-start | bytes 9437188
  285.6 9.4 %copy-start.1 = (f32[256,768]{0,1:T(8,128)S(1)}, f32[256,768]{0,1:T(8,128)}, u32[]{:S(2)}) copy-start(f32[256,768]{0,1:T(8,128)} %copy.20) | copy-start | bytes 2359300
  285.6 9.4 %copy-start.2 = (f32[96,8,2,128]{3,1,2,0:T(8,128)S(1)}, f32[96,8,2,128]{3,1,2,0:T(8,128)}, u32[]{:S(2)}) copy-start(f32[96,8,2,128]{3,1,2,0:T(8,128)} %copy.54) | copy-start | bytes 2359300
Sparse Core Ops, SparseCore 0:
  20.0 30.9 all-gather.3
  180.9 46.8 all-gather.7
  229.4 45.6 all-gather.5
Sparse Core Ops, SparseCore 1:
  84.9 85.6 all-reduce.2
  178.6 86.6 all-reduce.4
